TPU v7x, 32 devices: a whole 2x2x4 slice. The times are simulated.
32 devices in a mesh: row: 8 (over y, x, core), col: 4 (over z).
Axes of the slice: x: 2, y: 2, z: 4, core: 2. Of those that a mesh axis runs over, the one named last changes fastest.
Arguments:
- inverse_tiles: float32 [512, 512], P('row', 'col'), may hold values from -0.375 to 0.375
- factor_panels: float32 [3, 512, 256], P(None, 'row', 'col'), may hold values from -6 to 6
- block_rows: int32 [3, 8], replicated, may hold values from 0 to 15, as said below
- couplings: float32 [2, 512, 512], replicated, may hold values from -0.25 to 0.25
Outputs:
- new_columns: float32 [3, 512, 512], P(None, ('row', 'col'))
Inputs may be any that keep to these rules, and one draw needn't show every extreme that they name: `block_rows`: each row lists 8 different row blocks in no particular order; in each row, all 4 blocks q * 4 to q * 4 + 3 of some q are listed.
All inputs are finite; a program needn't handle non-finite values.
Results may differ from a plain program's by a relative error of at most 0.0001.
Values sent between devices are 32-bit elements; how exact they have to be, the bound alone decides.
No kernel may reach another device: no remote copies, remote signals or barrier semaphores. Data moves between devices by JAX's collectives and lax.ppermute only.
A program may use at most 64 MiB of HBM per device.

v0:
```python
import jax
import jax.numpy as jnp
from jax import lax
from jax.sharding import PartitionSpec as P


def on_device(inverse_tiles, factor_panels, block_rows, couplings):
    tile_rows, tile_cols = inverse_tiles.shape
    piece_rows = factor_panels.shape[1]
    listed = block_rows.shape[1]
    col_count = lax.axis_size("col")
    block_size = factor_panels.shape[2] * col_count // listed
    local_blocks = tile_cols // block_size
    my_column = lax.axis_index("col")
    offset = my_column * local_blocks
    targets = offset + jnp.arange(local_blocks, dtype=jnp.int32)
    results = []
    previous = None
    for section in range(factor_panels.shape[0]):
        section_rows = block_rows[section]
        gathered = lax.all_gather(factor_panels[section], "col", axis=1, tiled=True)
        onehot = (section_rows[:, None] == targets[None, :]).astype(jnp.float32)
        picked = jnp.einsum(
            "wpr,pq->wqr",
            gathered.reshape(piece_rows, listed, block_size),
            onehot,
            precision=lax.Precision.HIGHEST,
        ).reshape(piece_rows, tile_cols)
        partial_value = lax.dot_general(
            inverse_tiles,
            lax.all_gather(picked, "row", axis=0, tiled=True),
            (((1,), (1,)), ((), ())),
            precision=lax.Precision.HIGHEST,
            preferred_element_type=jnp.float32,
        )
        summed = lax.psum_scatter(partial_value, "col", scatter_dimension=0, tiled=True)
        if previous is not None:
            summed = summed + jnp.dot(
                previous,
                couplings[section - 1],
                precision=lax.Precision.HIGHEST,
                preferred_element_type=jnp.float32,
            )
        previous = -summed
        results.append(previous)
    return jnp.stack(results)


def solution(mesh):
    return jax.shard_map(
        on_device,
        mesh=mesh,
        in_specs=(P("row", "col"), P(None, "row", "col"), P(), P()),
        out_specs=P(None, ("row", "col"), None),
        check_vma=False,
    )
```

profile of v0, /device:TPU:0, one launch (start us, length us, event | category | flops | bytes accessed | tf_op | source)
XLA Modules:
  0.0 111.6 jit_solution(15987718816973304762)
XLA Ops:
  6.5 0.8 fusion.23
  7.3 0.1 copy.26
  7.4 15.1 %all-gather = f32[1,64,256]{1,2,0:T(8,128)S(1)} all-gather(f32[1,64,64]{1,2,0:T(8,128)S(1)} %copy.26), channel_id=2, replica_groups=mesh['row'=8,'col'=4] {'col'}, dimensions={2}, use_global_device_ids=true | all-gather | bytes 81920 | tf_op jit(solution)/shard_map/all_gather | solution.py:21
  22.5 0.8 slice_bitcast_fusion.2
  23.3 0.3 convolution_bitcast_fusion.5
  23.6 0.1 copy.17
  23.7 9.4 %all_gather.19 = f32[512,128]{1,0:T(8,128)S(1)} all-gather(f32[64,128]{1,0:T(8,128)S(1)} %copy.17), channel_id=1, replica_groups=mesh['row'=8,'col'=4] {'row'}, dimensions={0}, use_global_device_ids=true | all-gather | bytes 294912 | tf_op jit(solution)/shard_map/all_gather | solution.py:31
  33.1 1.1 convolution_bitcast_fusion.2
  34.3 0.1 copy.27
  34.3 13.5 %all-gather.1 = f32[1,64,256]{1,2,0:T(8,128)S(1)} all-gather(f32[1,64,64]{1,2,0:T(8,128)S(1)} %copy.27), channel_id=3, replica_groups=mesh['row'=8,'col'=4] {'col'}, dimensions={2}, use_global_device_ids=true | all-gather | bytes 81920 | tf_op jit(solution)/shard_map/all_gather | solution.py:21
  47.9 0.3 convolution_bitcast_fusion.4
  48.2 0.1 copy.21
  48.2 9.3 %all_gather.21 = f32[512,128]{1,0:T(8,128)S(1)} all-gather(f32[64,128]{1,0:T(8,128)S(1)} %copy.21), channel_id=1, replica_groups=mesh['row'=8,'col'=4] {'row'}, dimensions={0}, use_global_device_ids=true | all-gather | bytes 294912 | tf_op jit(solution)/shard_map/all_gather | solution.py:31
  57.5 1.1 convolution_bitcast_fusion.1
  58.6 0.1 copy.28
  58.7 13.7 %all-gather.2 = f32[1,64,256]{1,2,0:T(8,128)S(1)} all-gather(f32[1,64,64]{1,2,0:T(8,128)S(1)} %copy.28), channel_id=4, replica_groups=mesh['row'=8,'col'=4] {'col'}, dimensions={2}, use_global_device_ids=true | all-gather | bytes 81920 | tf_op jit(solution)/shard_map/all_gather | solution.py:21
  72.4 0.3 convolution_bitcast_fusion.3
  72.8 8.7 %all_gather.23 = f32[512,128]{1,0:T(8,128)S(1)} all-gather(f32[64,128]{1,0:T(8,128)S(1)} %copy.25), channel_id=1, replica_groups=mesh['row'=8,'col'=4] {'row'}, dimensions={0}, use_global_device_ids=true | all-gather | bytes 294912 | tf_op jit(solution)/shard_map/all_gather | solution.py:31
  81.5 1.1 convolution_bitcast_fusion
  82.7 0.8 negate_bitcast_fusion
  83.4 1.4 %fusion.2 = f32[16,512]{1,0:T(8,128)S(1)} fusion(f32[16,512]{1,0:T(8,128)} %reduce-scatter.6.cloned.1.call-done, f32[2,512,512]{2,1,0:T(8,128)S(1)} %copy-done.1, f32[16,512]{1,0:T(8,128)} %reduce-scatter.4.cloned.1.call-done), kind=kOutput, calls=%fused_computation.10 | convolution fusion | flops 50356224 | bytes 1146880 | tf_op jit(solution)/shard_map/dot_general | solution.py:38
  84.8 18.2 %reduce-scatter.8.cloned.1.call-done = f32[16,512]{1,0:T(8,128)} async-done(((f32[64,512]{1,0:T(8,128)}), f32[16,512]{1,0:T(8,128)}) %reduce-scatter.8.cloned.1.call-update) | async-done | bytes 32784 | tf_op jit(solution)/shard_map/reduce_scatter | solution.py:36
  103.0 1.4 %fusion.1 = f32[1,16,512]{2,1,0:T(8,128)S(1)} fusion(f32[16,512]{1,0:T(8,128)} %reduce-scatter.8.cloned.1.call-done, f32[16,512]{1,0:T(8,128)S(1)} %fusion.2, f32[2,512,512]{2,1,0:T(8,128)S(1)} %copy-done.1), kind=kOutput, calls=%fused_computation.8 | convolution fusion | flops 50348032 | bytes 1146880 | tf_op jit(solution)/shard_map/dot_general | solution.py:38
  104.4 0.6 pad_maximum_fusion
  (17 shorter events, 0.3 us)
Async XLA Ops:
  6.5 26.6 %copy-start = (f32[64,128]{1,0:T(8,128)S(1)}, f32[64,128]{1,0:T(8,128)}, u32[]{:S(2)}) copy-start(f32[64,128]{1,0:T(8,128)} %param.4) | copy-start | bytes 98308
  6.5 76.1 %reduce-scatter.4.cloned.1.call-start = ((), (), s32[]{:S(2)}) async-start(), calls=%async_computation.3 | async-start | bytes 163840 | tf_op jit(solution)/shard_map/reduce_scatter | solution.py:36
  23.6 59.9 %copy-start.1 = (f32[2,512,512]{2,1,0:T(8,128)S(1)}, f32[2,512,512]{2,1,0:T(8,128)}, u32[]{:S(2)}) copy-start(f32[2,512,512]{2,1,0:T(8,128)} %param.7) | copy-start | bytes 6291460
  34.2 49.2 %reduce-scatter.6.cloned.1.call-start = ((), (), s32[]{:S(2)}) async-start(), calls=%async_computation.4 | async-start | bytes 163840 | tf_op jit(solution)/shard_map/reduce_scatter | solution.py:36
  58.6 44.4 %reduce-scatter.8.cloned.1.call-start = ((), (), s32[]{:S(2)}) async-start(), calls=%async_computation.5 | async-start | bytes 163840 | tf_op jit(solution)/shard_map/reduce_scatter | solution.py:36
Sparse Core Ops, SparseCore 0:
  34.3 19.9 reduce-scatter.3
  58.7 20.2 reduce-scatter.5
  82.8 20.2 reduce-scatter.7
where the time goes:
time: 112 us
  blocking collectives  69.8 us (62%)
  waiting for transfers between devices  18.3 us (16%)
  between operations  13.2 us (12%)
  matrix products  6.76 us (6%)
  local copies, waits for them, and re-layouts  2.04 us (2%)
  other arithmetic  1.41 us (1%)
    all_gather x3, blocking collectives, on_device(): gathered = lax.all_gather(factor_panels[section], 'col', axis=1, tiled=True)  42.3 us
    all_gather x3, blocking collectives, on_device(): lax.all_gather(picked, 'row', axis=0, tiled=True)  27.5 us
    reduce_scatter x3, waiting for transfers between devices, on_device(): lax.psum_scatter(partial_value, 'col', scatter_dimension=0, tiled=True)  18.2 us
    dot_general x3, matrix products, on_device(): lax.dot_general(inverse_tiles, lax.all_gather(picked, 'row', axis=0, tile...  3.21 us
    dot_general x2, matrix products, on_device(): jnp.dot(previous, couplings[section - 1], precision=lax.Precision.HIGHEST...  2.76 us
  transfers between devices with their start and end apart: 3, of which 1 were waited for; matrix products, arithmetic and copies ran while one was open for 5% of the time, Pallas kernels for 0%

commit v1 on v0

--- a/solution.py
+++ b/solution.py
@@ -2,6 +2,23 @@
 import jax.numpy as jnp
 from jax import lax
 from jax.sharding import PartitionSpec as P
+
+
+def laid_out(parts, dim):
+    parts = jnp.moveaxis(parts, 0, dim)
+    shape = parts.shape
+    return parts.reshape(*shape[:dim], shape[dim] * shape[dim + 1], *shape[dim + 2 :])
+
+
+def gather_around(array, axis, dim):
+    count = lax.axis_size(axis)
+    right = [(i, (i + 1) % count) for i in range(count)]
+    parts = [array]
+    while len(parts) < count:
+        parts.append(lax.ppermute(parts[-1], axis, right))
+    position = lax.axis_index(axis)
+    parts = jnp.stack(parts)[(position - jnp.arange(count)) % count]
+    return laid_out(parts, dim)
 
 
 def on_device(inverse_tiles, factor_panels, block_rows, couplings):
@@ -28,7 +45,7 @@
         ).reshape(piece_rows, tile_cols)
         partial_value = lax.dot_general(
             inverse_tiles,
-            lax.all_gather(picked, "row", axis=0, tiled=True),
+            gather_around(picked, "row", 0),
             (((1,), (1,)), ((), ())),
             precision=lax.Precision.HIGHEST,
             preferred_element_type=jnp.float32,

time: 112 us -> 151 us (1.35)
  waiting for transfers between devices: 18.3 us -> 73.7 us
  blocking collectives: 69.8 us -> 42.2 us
  local copies, waits for them, and re-layouts: 2.04 us -> 11.1 us
  starting transfers between devices: 0.09 us -> 2.03 us
    reduce_scatter x3, waiting for transfers between devices: 18.2 us -> 51.7 us  [on_device(): lax.psum_scatter(partial_value, 'col', scatter_dimension=0, tiled=True)]
    all_gather x3 -> x0, blocking collectives: 27.5 us -> none  [on_device(): lax.all_gather(picked, 'row', axis=0, tiled=True)]
    ppermute x0 -> x21, waiting for transfers between devices: none -> 22 us  [gather_around(): parts.append(lax.ppermute(parts[-1], axis, right))]
    unnamed x7 -> x28, local copies, waits for them, and re-layouts: 0.23 us -> 4.67 us
    gather x0 -> x6, local copies, waits for them, and re-layouts: none -> 3.32 us  [gather_around(): parts = jnp.stack(parts)[(position - jnp.arange(count)) % count]]
    ppermute x0 -> x21, starting transfers between devices: none -> 1.94 us  [gather_around(): parts.append(lax.ppermute(parts[-1], axis, right))]
  transfers between devices with their start and end apart: 3 -> 24, of which waited for: 1 -> 20; matrix products, arithmetic and copies ran while one was open for 5% -> 10% of each run, Pallas kernels for 0% -> 0%
where the time goes in v1:
time: 151 us
  waiting for transfers between devices  73.7 us (49%)
  blocking collectives  42.2 us (28%)
  between operations  13.3 us (9%)
  local copies, waits for them, and re-layouts  11.1 us (7%)
  matrix products  6.77 us (4%)
  starting transfers between devices  2.03 us (1%)
    reduce_scatter x3, waiting for transfers between devices, on_device(): lax.psum_scatter(partial_value, 'col', scatter_dimension=0, tiled=True)  51.7 us
    all_gather x3, blocking collectives, on_device(): gathered = lax.all_gather(factor_panels[section], 'col', axis=1, tiled=True)  42.2 us
    ppermute x21, waiting for transfers between devices, gather_around(): parts.append(lax.ppermute(parts[-1], axis, right))  22 us
    unnamed x28, local copies, waits for them, and re-layouts  4.67 us
    gather x6, local copies, waits for them, and re-layouts, gather_around(): parts = jnp.stack(parts)[(position - jnp.arange(count)) % count]  3.32 us
    dot_general x3, matrix products, on_device(): lax.dot_general(inverse_tiles, gather_around(picked, 'row', 0), (((1,), (...  3.21 us
  transfers between devices with their start and end apart: 24, of which 20 were waited for; matrix products, arithmetic and copies ran while one was open for 10% of the time, Pallas kernels for 0%

profile of v1, /device:TPU:0, one launch (start us, length us, event | category | flops | bytes accessed | tf_op | source)
XLA Modules:
  0.0 150.5 jit_solution(3081522991504149923)
XLA Ops:
  7.4 15.1 %all-gather = f32[1,64,256]{1,2,0:T(8,128)S(1)} all-gather(f32[1,64,64]{1,2,0:T(8,128)S(1)} %copy.32), channel_id=2, replica_groups=mesh['row'=8,'col'=4] {'col'}, dimensions={2}, use_global_device_ids=true | all-gather | bytes 81920 | tf_op jit(solution)/shard_map/all_gather | solution.py:38
  23.7 13.6 %all-gather.1 = f32[1,64,256]{1,2,0:T(8,128)S(1)} all-gather(f32[1,64,64]{1,2,0:T(8,128)S(1)} %copy.33), channel_id=3, replica_groups=mesh['row'=8,'col'=4] {'col'}, dimensions={2}, use_global_device_ids=true | all-gather | bytes 81920 | tf_op jit(solution)/shard_map/all_gather | solution.py:38
  37.8 13.5 %all-gather.2 = f32[1,64,256]{1,2,0:T(8,128)S(1)} all-gather(f32[1,64,64]{1,2,0:T(8,128)S(1)} %copy.34), channel_id=4, replica_groups=mesh['row'=8,'col'=4] {'col'}, dimensions={2}, use_global_device_ids=true | all-gather | bytes 81920 | tf_op jit(solution)/shard_map/all_gather | solution.py:38
  52.3 1.6 %collective-permute-start.1 = (f32[64,128]{0,1:T(8,128)S(1)}, f32[64,128]{0,1:T(8,128)S(1)}, u32[]{:S(2)}, u32[]{:S(2)}) collective-permute-start(f32[64,128]{0,1:T(8,128)S(1)} %collective-permute-done), channel_id=1, source_target_pairs={{0,4},{4,8},{8,12},{12,16},{16,20},{20,24},{24,28},{28,0},{1,5},{5... | collective-permute-start | bytes 98312 | tf_op jit(solution)/shard_map/ppermute | solution.py:18
  54.6 1.6 %collective-permute-done.14 = f32[64,128]{0,1:T(8,128)S(1)} collective-permute-done((f32[64,128]{0,1:T(8,128)S(1)}, f32[64,128]{0,1:T(8,128)S(1)}, u32[]{:S(2)}, u32[]{:S(2)}) %collective-permute-start.14) | collective-permute-done | bytes 32800 | tf_op jit(solution)/shard_map/ppermute | solution.py:18
  57.0 1.6 %collective-permute-done.8 = f32[64,128]{0,1:T(8,128)S(1)} collective-permute-done((f32[64,128]{0,1:T(8,128)S(1)}, f32[64,128]{0,1:T(8,128)S(1)}, u32[]{:S(2)}, u32[]{:S(2)}) %collective-permute-start.8) | collective-permute-done | bytes 32800 | tf_op jit(solution)/shard_map/ppermute | solution.py:18
  59.2 1.6 %collective-permute-done.15 = f32[64,128]{0,1:T(8,128)S(1)} collective-permute-done((f32[64,128]{0,1:T(8,128)S(1)}, f32[64,128]{0,1:T(8,128)S(1)}, u32[]{:S(2)}, u32[]{:S(2)}) %collective-permute-start.15) | collective-permute-done | bytes 32800 | tf_op jit(solution)/shard_map/ppermute | solution.py:18
  61.5 1.6 %collective-permute-done.9 = f32[64,128]{0,1:T(8,128)S(1)} collective-permute-done((f32[64,128]{0,1:T(8,128)S(1)}, f32[64,128]{0,1:T(8,128)S(1)}, u32[]{:S(2)}, u32[]{:S(2)}) %collective-permute-start.9) | collective-permute-done | bytes 32800 | tf_op jit(solution)/shard_map/ppermute | solution.py:18
  63.8 1.6 %collective-permute-done.16 = f32[64,128]{0,1:T(8,128)S(1)} collective-permute-done((f32[64,128]{0,1:T(8,128)S(1)}, f32[64,128]{0,1:T(8,128)S(1)}, u32[]{:S(2)}, u32[]{:S(2)}) %collective-permute-start.16) | collective-permute-done | bytes 32800 | tf_op jit(solution)/shard_map/ppermute | solution.py:18
  66.1 1.6 %collective-permute-done.10 = f32[64,128]{0,1:T(8,128)S(1)} collective-permute-done((f32[64,128]{0,1:T(8,128)S(1)}, f32[64,128]{0,1:T(8,128)S(1)}, u32[]{:S(2)}, u32[]{:S(2)}) %collective-permute-start.10) | collective-permute-done | bytes 32800 | tf_op jit(solution)/shard_map/ppermute | solution.py:18
  68.4 1.6 %collective-permute-done.17 = f32[64,128]{0,1:T(8,128)S(1)} collective-permute-done((f32[64,128]{0,1:T(8,128)S(1)}, f32[64,128]{0,1:T(8,128)S(1)}, u32[]{:S(2)}, u32[]{:S(2)}) %collective-permute-start.17) | collective-permute-done | bytes 32800 | tf_op jit(solution)/shard_map/ppermute | solution.py:18
  70.7 1.6 %collective-permute-done.11 = f32[64,128]{0,1:T(8,128)S(1)} collective-permute-done((f32[64,128]{0,1:T(8,128)S(1)}, f32[64,128]{0,1:T(8,128)S(1)}, u32[]{:S(2)}, u32[]{:S(2)}) %collective-permute-start.11) | collective-permute-done | bytes 32800 | tf_op jit(solution)/shard_map/ppermute | solution.py:18
  73.0 1.6 %collective-permute-done.18 = f32[64,128]{0,1:T(8,128)S(1)} collective-permute-done((f32[64,128]{0,1:T(8,128)S(1)}, f32[64,128]{0,1:T(8,128)S(1)}, u32[]{:S(2)}, u32[]{:S(2)}) %collective-permute-start.18) | collective-permute-done | bytes 32800 | tf_op jit(solution)/shard_map/ppermute | solution.py:18
  75.3 1.6 %collective-permute-done.12 = f32[64,128]{0,1:T(8,128)S(1)} collective-permute-done((f32[64,128]{0,1:T(8,128)S(1)}, f32[64,128]{0,1:T(8,128)S(1)}, u32[]{:S(2)}, u32[]{:S(2)}) %collective-permute-start.12) | collective-permute-done | bytes 32800 | tf_op jit(solution)/shard_map/ppermute | solution.py:18
  77.6 1.6 %collective-permute-done.19 = f32[64,128]{0,1:T(8,128)S(1)} collective-permute-done((f32[64,128]{0,1:T(8,128)S(1)}, f32[64,128]{0,1:T(8,128)S(1)}, u32[]{:S(2)}, u32[]{:S(2)}) %collective-permute-start.19) | collective-permute-done | bytes 32800 | tf_op jit(solution)/shard_map/ppermute | solution.py:18
  80.7 1.1 convolution_bitcast_fusion.2
  82.5 1.6 %gather_fusion.1 = f32[8,64,128]{1,2,0:T(8,128)S(1)} fusion(f32[8,64,128]{1,2,0:T(8,128)} %bitcast_dynamic-update-slice_fusion.7, s32[1024]{0:T(1024)S(1)} %pad_clamp_fusion), kind=kCustom, calls=%fused_computation.1 | custom fusion | bytes 524320 | tf_op jit(solution)/shard_map/gather | solution.py:20
  84.3 1.1 convolution_bitcast_fusion.1
  87.1 1.1 convolution_bitcast_fusion
  88.2 14.0 %reduce-scatter.4.cloned.1.call-done = f32[16,512]{1,0:T(8,128)} async-done(((f32[64,512]{1,0:T(8,128)}), f32[16,512]{1,0:T(8,128)}) %reduce-scatter.4.cloned.1.call-update) | async-done | bytes 32784 | tf_op jit(solution)/shard_map/reduce_scatter | solution.py:53
  102.9 19.1 %reduce-scatter.6.cloned.1.call-done = f32[16,512]{1,0:T(8,128)} async-done(((f32[64,512]{1,0:T(8,128)}), f32[16,512]{1,0:T(8,128)}) %reduce-scatter.6.cloned.1.call-update) | async-done | bytes 32784 | tf_op jit(solution)/shard_map/reduce_scatter | solution.py:53
  122.1 1.4 fusion.2
  123.4 18.5 %reduce-scatter.8.cloned.1.call-done = f32[16,512]{1,0:T(8,128)} async-done(((f32[64,512]{1,0:T(8,128)}), f32[16,512]{1,0:T(8,128)}) %reduce-scatter.8.cloned.1.call-update) | async-done | bytes 32784 | tf_op jit(solution)/shard_map/reduce_scatter | solution.py:53
  142.0 1.4 fusion.1
  (85 shorter events, 16.6 us)
Async XLA Ops:
  6.5 95.6 %reduce-scatter.4.cloned.1.call-start = ((), (), s32[]{:S(2)}) async-start(), calls=%async_computation.3 | async-start | bytes 163840 | tf_op jit(solution)/shard_map/reduce_scatter | solution.py:53
  23.6 28.7 %collective-permute-start = (f32[64,128]{0,1:T(8,128)S(1)}, f32[64,128]{0,1:T(8,128)S(1)}, u32[]{:S(2)}, u32[]{:S(2)}) collective-permute-start(f32[64,128]{0,1:T(8,128)S(1)} %bitcast.108), channel_id=1, source_target_pairs={{0,4},{4,8},{8,12},{12,16},{16,20},{20,24},{24,28},{28,0},{1,5},{5... | collective-permute-start | bytes 98312 | tf_op jit(solution)/shard_map/ppermute | solution.py:18
  37.6 16.3 %collective-permute-start.7 = (f32[64,128]{0,1:T(8,128)S(1)}, f32[64,128]{0,1:T(8,128)S(1)}, u32[]{:S(2)}, u32[]{:S(2)}) collective-permute-start(f32[64,128]{0,1:T(8,128)S(1)} %bitcast.110), channel_id=1, source_target_pairs={{0,4},{4,8},{8,12},{12,16},{16,20},{20,24},{24,28},{28,0},{1,5},{5... | collective-permute-start | bytes 98312 | tf_op jit(solution)/shard_map/ppermute | solution.py:18
  51.6 4.6 %collective-permute-start.14 = (f32[64,128]{0,1:T(8,128)S(1)}, f32[64,128]{0,1:T(8,128)S(1)}, u32[]{:S(2)}, u32[]{:S(2)}) collective-permute-start(f32[64,128]{0,1:T(8,128)S(1)} %bitcast.112), channel_id=1, source_target_pairs={{0,4},{4,8},{8,12},{12,16},{16,20},{20,24},{24,28},{28,0},{1,5},{5... | collective-permute-start | bytes 98312 | tf_op jit(solution)/shard_map/ppermute | solution.py:18
  52.3 4.6 %collective-permute-start.1 = (f32[64,128]{0,1:T(8,128)S(1)}, f32[64,128]{0,1:T(8,128)S(1)}, u32[]{:S(2)}, u32[]{:S(2)}) collective-permute-start(f32[64,128]{0,1:T(8,128)S(1)} %collective-permute-done), channel_id=1, source_target_pairs={{0,4},{4,8},{8,12},{12,16},{16,20},{20,24},{24,28},{28,0},{1,5},{5... | collective-permute-start | bytes 98312 | tf_op jit(solution)/shard_map/ppermute | solution.py:18
  53.9 4.6 %collective-permute-start.8 = (f32[64,128]{0,1:T(8,128)S(1)}, f32[64,128]{0,1:T(8,128)S(1)}, u32[]{:S(2)}, u32[]{:S(2)}) collective-permute-start(f32[64,128]{0,1:T(8,128)S(1)} %collective-permute-done.7), channel_id=1, source_target_pairs={{0,4},{4,8},{8,12},{12,16},{16,20},{20,24},{24,28},{28,0},{1,5},{5... | collective-permute-start | bytes 98312 | tf_op jit(solution)/shard_map/ppermute | solution.py:18
  56.2 4.6 %collective-permute-start.15 = (f32[64,128]{0,1:T(8,128)S(1)}, f32[64,128]{0,1:T(8,128)S(1)}, u32[]{:S(2)}, u32[]{:S(2)}) collective-permute-start(f32[64,128]{0,1:T(8,128)S(1)} %collective-permute-done.14), channel_id=1, source_target_pairs={{0,4},{4,8},{8,12},{12,16},{16,20},{20,24},{24,28},{28,0},{1,5},{5... | collective-permute-start | bytes 98312 | tf_op jit(solution)/shard_map/ppermute | solution.py:18
  56.9 4.6 %collective-permute-start.2 = (f32[64,128]{0,1:T(8,128)S(1)}, f32[64,128]{0,1:T(8,128)S(1)}, u32[]{:S(2)}, u32[]{:S(2)}) collective-permute-start(f32[64,128]{0,1:T(8,128)S(1)} %collective-permute-done.1), channel_id=1, source_target_pairs={{0,4},{4,8},{8,12},{12,16},{16,20},{20,24},{24,28},{28,0},{1,5},{5... | collective-permute-start | bytes 98312 | tf_op jit(solution)/shard_map/ppermute | solution.py:18
  58.6 4.6 %collective-permute-start.9 = (f32[64,128]{0,1:T(8,128)S(1)}, f32[64,128]{0,1:T(8,128)S(1)}, u32[]{:S(2)}, u32[]{:S(2)}) collective-permute-start(f32[64,128]{0,1:T(8,128)S(1)} %collective-permute-done.8), channel_id=1, source_target_pairs={{0,4},{4,8},{8,12},{12,16},{16,20},{20,24},{24,28},{28,0},{1,5},{5... | collective-permute-start | bytes 98312 | tf_op jit(solution)/shard_map/ppermute | solution.py:18
  60.8 4.6 %collective-permute-start.16 = (f32[64,128]{0,1:T(8,128)S(1)}, f32[64,128]{0,1:T(8,128)S(1)}, u32[]{:S(2)}, u32[]{:S(2)}) collective-permute-start(f32[64,128]{0,1:T(8,128)S(1)} %collective-permute-done.15), channel_id=1, source_target_pairs={{0,4},{4,8},{8,12},{12,16},{16,20},{20,24},{24,28},{28,0},{1,5},{5... | collective-permute-start | bytes 98312 | tf_op jit(solution)/shard_map/ppermute | solution.py:18
  61.5 4.6 %collective-permute-start.3 = (f32[64,128]{0,1:T(8,128)S(1)}, f32[64,128]{0,1:T(8,128)S(1)}, u32[]{:S(2)}, u32[]{:S(2)}) collective-permute-start(f32[64,128]{0,1:T(8,128)S(1)} %collective-permute-done.2), channel_id=1, source_target_pairs={{0,4},{4,8},{8,12},{12,16},{16,20},{20,24},{24,28},{28,0},{1,5},{5... | collective-permute-start | bytes 98312 | tf_op jit(solution)/shard_map/ppermute | solution.py:18
  63.2 4.6 %collective-permute-start.10 = (f32[64,128]{0,1:T(8,128)S(1)}, f32[64,128]{0,1:T(8,128)S(1)}, u32[]{:S(2)}, u32[]{:S(2)}) collective-permute-start(f32[64,128]{0,1:T(8,128)S(1)} %collective-permute-done.9), channel_id=1, source_target_pairs={{0,4},{4,8},{8,12},{12,16},{16,20},{20,24},{24,28},{28,0},{1,5},{5... | collective-permute-start | bytes 98312 | tf_op jit(solution)/shard_map/ppermute | solution.py:18
  65.4 4.6 %collective-permute-start.17 = (f32[64,128]{0,1:T(8,128)S(1)}, f32[64,128]{0,1:T(8,128)S(1)}, u32[]{:S(2)}, u32[]{:S(2)}) collective-permute-start(f32[64,128]{0,1:T(8,128)S(1)} %collective-permute-done.16), channel_id=1, source_target_pairs={{0,4},{4,8},{8,12},{12,16},{16,20},{20,24},{24,28},{28,0},{1,5},{5... | collective-permute-start | bytes 98312 | tf_op jit(solution)/shard_map/ppermute | solution.py:18
  66.1 4.6 %collective-permute-start.4 = (f32[64,128]{0,1:T(8,128)S(1)}, f32[64,128]{0,1:T(8,128)S(1)}, u32[]{:S(2)}, u32[]{:S(2)}) collective-permute-start(f32[64,128]{0,1:T(8,128)S(1)} %collective-permute-done.3), channel_id=1, source_target_pairs={{0,4},{4,8},{8,12},{12,16},{16,20},{20,24},{24,28},{28,0},{1,5},{5... | collective-permute-start | bytes 98312 | tf_op jit(solution)/shard_map/ppermute | solution.py:18
  67.8 4.6 %collective-permute-start.11 = (f32[64,128]{0,1:T(8,128)S(1)}, f32[64,128]{0,1:T(8,128)S(1)}, u32[]{:S(2)}, u32[]{:S(2)}) collective-permute-start(f32[64,128]{0,1:T(8,128)S(1)} %collective-permute-done.10), channel_id=1, source_target_pairs={{0,4},{4,8},{8,12},{12,16},{16,20},{20,24},{24,28},{28,0},{1,5},{5... | collective-permute-start | bytes 98312 | tf_op jit(solution)/shard_map/ppermute | solution.py:18
  70.0 4.6 %collective-permute-start.18 = (f32[64,128]{0,1:T(8,128)S(1)}, f32[64,128]{0,1:T(8,128)S(1)}, u32[]{:S(2)}, u32[]{:S(2)}) collective-permute-start(f32[64,128]{0,1:T(8,128)S(1)} %collective-permute-done.17), channel_id=1, source_target_pairs={{0,4},{4,8},{8,12},{12,16},{16,20},{20,24},{24,28},{28,0},{1,5},{5... | collective-permute-start | bytes 98312 | tf_op jit(solution)/shard_map/ppermute | solution.py:18
  70.7 4.6 %collective-permute-start.5 = (f32[64,128]{0,1:T(8,128)S(1)}, f32[64,128]{0,1:T(8,128)S(1)}, u32[]{:S(2)}, u32[]{:S(2)}) collective-permute-start(f32[64,128]{0,1:T(8,128)S(1)} %collective-permute-done.4), channel_id=1, source_target_pairs={{0,4},{4,8},{8,12},{12,16},{16,20},{20,24},{24,28},{28,0},{1,5},{5... | collective-permute-start | bytes 98312 | tf_op jit(solution)/shard_map/ppermute | solution.py:18
  72.4 4.6 %collective-permute-start.12 = (f32[64,128]{0,1:T(8,128)S(1)}, f32[64,128]{0,1:T(8,128)S(1)}, u32[]{:S(2)}, u32[]{:S(2)}) collective-permute-start(f32[64,128]{0,1:T(8,128)S(1)} %collective-permute-done.11), channel_id=1, source_target_pairs={{0,4},{4,8},{8,12},{12,16},{16,20},{20,24},{24,28},{28,0},{1,5},{5... | collective-permute-start | bytes 98312 | tf_op jit(solution)/shard_map/ppermute | solution.py:18
  74.6 4.6 %collective-permute-start.19 = (f32[64,128]{0,1:T(8,128)S(1)}, f32[64,128]{0,1:T(8,128)S(1)}, u32[]{:S(2)}, u32[]{:S(2)}) collective-permute-start(f32[64,128]{0,1:T(8,128)S(1)} %collective-permute-done.18), channel_id=1, source_target_pairs={{0,4},{4,8},{8,12},{12,16},{16,20},{20,24},{24,28},{28,0},{1,5},{5... | collective-permute-start | bytes 98312 | tf_op jit(solution)/shard_map/ppermute | solution.py:18
  75.3 4.6 %collective-permute-start.6 = (f32[64,128]{0,1:T(8,128)S(1)}, f32[64,128]{0,1:T(8,128)S(1)}, u32[]{:S(2)}, u32[]{:S(2)}) collective-permute-start(f32[64,128]{0,1:T(8,128)S(1)} %collective-permute-done.5), channel_id=1, source_target_pairs={{0,4},{4,8},{8,12},{12,16},{16,20},{20,24},{24,28},{28,0},{1,5},{5... | collective-permute-start | bytes 98312 | tf_op jit(solution)/shard_map/ppermute | solution.py:18
  76.9 4.9 %collective-permute-start.13 = (f32[64,128]{0,1:T(8,128)S(1)}, f32[64,128]{0,1:T(8,128)S(1)}, u32[]{:S(2)}, u32[]{:S(2)}) collective-permute-start(f32[64,128]{0,1:T(8,128)S(1)} %collective-permute-done.12), channel_id=1, source_target_pairs={{0,4},{4,8},{8,12},{12,16},{16,20},{20,24},{24,28},{28,0},{1,5},{5... | collective-permute-start | bytes 98312 | tf_op jit(solution)/shard_map/ppermute | solution.py:18
  79.1 6.3 %collective-permute-start.20 = (f32[64,128]{0,1:T(8,128)S(1)}, f32[64,128]{0,1:T(8,128)}, u32[]{:S(2)}, u32[]{:S(2)}) collective-permute-start(f32[64,128]{0,1:T(8,128)S(1)} %collective-permute-done.19), channel_id=1, source_target_pairs={{0,4},{4,8},{8,12},{12,16},{16,20},{20,24},{24,28},{28,0},{1,5},{5... | collective-permute-start | bytes 98312 | tf_op jit(solution)/shard_map/ppermute | solution.py:18
  81.8 40.3 %reduce-scatter.6.cloned.1.call-start = ((), (), s32[]{:S(2)}) async-start(), calls=%async_computation.4 | async-start | bytes 163840 | tf_op jit(solution)/shard_map/reduce_scatter | solution.py:53
  85.4 56.6 %reduce-scatter.8.cloned.1.call-start = ((), (), s32[]{:S(2)}) async-start(), calls=%async_computation.5 | async-start | bytes 163840 | tf_op jit(solution)/shard_map/reduce_scatter | solution.py:53
  (2 other events, 114.4 us)
Sparse Core Ops, SparseCore 0:
  81.9 20.1 reduce-scatter.3
  104.4 17.6 reduce-scatter.5
  124.3 17.6 reduce-scatter.7
